TPU v7x, 32 devices: a whole 2x2x4 slice. The times are simulated.
32 devices in a mesh: side: 2 (over core), group: 8 (over z, y), head: 2 (over x).
Axes of the slice: x: 2, y: 2, z: 4, core: 2. Of those that a mesh axis runs over, the one named last changes fastest.
Arguments:
- pool_rows: bfloat16 [2, 768, 4096], P('side', ('group', 'head')), may hold values from -24 to 24
- pool_weight: bfloat16 [2, 4096, 8192], P('side', 'group', 'head'), as said below
- lengths: int32 [8, 3], replicated, may hold values from 1 to 48, 96 in all within a row
- owner: int32 [8, 3], replicated, may hold values from 0 to 7, as said below
Outputs:
- pool_out: bfloat16 [2, 768, 4096], P('side', 'group', 'head')
Inputs may be any that keep to these rules, and one draw needn't show every extreme that they name: owner[p, j] is p with the binary digits of m_j flipped, where m_j = owner[0, j] is the same for every p; the m_j differ between slots, and every binary digit below 8 is set in some m_j. So the 3 requests of a prefill group go to different decode groups, and every decode group receives exactly one request for each slot j. `lengths`: each row sums to 96. `pool_weight`: independent normal entries of deviation 1 / sqrt(4096).
All inputs are finite; a program needn't handle non-finite values.
Results may differ from a plain program's by a relative error of at most 0.0061.
Values may be sent and summed in bfloat16 or wider, within the bound.
A program may use at most 128 MiB of HBM per device.

v0:
```python
import jax
import jax.numpy as jnp
from jax import lax
from jax.sharding import PartitionSpec as P

HEAD_DIM = 256


def shifted(value, axis, by):
    count = lax.axis_size(axis)
    pairs = [(i, i + by) for i in range(count) if 0 <= i + by < count]
    return lax.ppermute(value, axis, pairs)


def on_device(pool_rows, pool_weight, lengths, owner):
    side_index = lax.axis_index("side")
    group_index = lax.axis_index("group")
    requests = lengths.shape[1]
    gathered = lax.all_gather(pool_rows[0], "head", axis=0, tiled=True)
    weight = lax.all_gather(pool_weight[0], "group", axis=0, tiled=True)
    mem_g = gathered.shape[0]
    wide = weight.shape[1] // 2
    heads_dev = wide // HEAD_DIM
    q_req = mem_g // requests
    scale = 1.0 / HEAD_DIM**0.5
    cached = jnp.dot(gathered, weight, preferred_element_type=jnp.float32).astype(jnp.bfloat16)
    queries = cached[:, :wide]
    starts = jnp.cumsum(lengths, axis=1) - lengths
    groups = jnp.arange(lengths.shape[0], dtype=jnp.int32)
    sources, begins, counts = ([], [], [])
    for slot in range(requests):
        hit = owner[:, slot] == group_index
        sources.append(jnp.sum(jnp.where(hit, groups, 0)))
        begins.append(jnp.sum(jnp.where(hit, starts[:, slot], 0)))
        counts.append(jnp.sum(jnp.where(hit, lengths[:, slot], 0)))
    moved = shifted(cached, "side", 1)
    row_slot = jnp.arange(mem_g, dtype=jnp.int32) // q_req
    lower = jnp.zeros((mem_g,), jnp.int32)
    upper = jnp.zeros((mem_g,), jnp.int32)
    for slot in range(requests):
        here = row_slot == slot
        first_row = sources[slot] * mem_g + begins[slot]
        lower = jnp.where(here, first_row, lower)
        upper = jnp.where(here, first_row + counts[slot], upper)
    query_heads = queries.reshape(mem_g, heads_dev, HEAD_DIM)
    piece = lax.all_gather(moved, "group", axis=0, tiled=True)
    running = jnp.full((heads_dev, mem_g), -1e30, jnp.float32)
    count_rows = piece.shape[0]
    key_index = jnp.arange(count_rows, dtype=jnp.int32)
    key_rows = piece[:, :wide].reshape(count_rows, heads_dev, HEAD_DIM)
    value_rows = piece[:, wide:].reshape(count_rows, heads_dev, HEAD_DIM)
    allowed = (key_index[None, :] >= lower[:, None]) & (key_index[None, :] < upper[:, None])
    scores = (
        jnp.einsum("qeh,keh->eqk", query_heads, key_rows, preferred_element_type=jnp.float32)
        * scale
    )
    scores = jnp.where(allowed[None], scores, -1e30)
    newest = jnp.maximum(running, jnp.max(scores, axis=-1))
    expo = jnp.where(allowed[None], jnp.exp(scores - newest[:, :, None]), 0.0)
    total = jnp.sum(expo, axis=-1)
    update = jnp.einsum(
        "eqk,keh->eqh", expo.astype(jnp.bfloat16), value_rows, preferred_element_type=jnp.float32
    )
    accum = update
    running, total, accum = (newest, total, accum)
    mixed = accum / total[:, :, None]
    attended = jnp.transpose(mixed, (1, 0, 2)).reshape(mem_g, wide).astype(jnp.bfloat16)
    partial_out = lax.dot_general(
        attended, weight[:, wide:], (((1,), (1,)), ((), ())), preferred_element_type=jnp.float32
    )
    decoded = lax.psum_scatter(partial_out, "head", scatter_dimension=1, tiled=True).astype(
        jnp.bfloat16
    )
    result = jnp.where(side_index == 0, cached[:, :wide], decoded)
    return result[None]


def solution(mesh):
    placed = (P("side", ("group", "head"), None), P("side", "group", "head"), P(), P())
    return jax.shard_map(
        on_device, mesh=mesh, in_specs=placed, out_specs=P("side", "group", "head"), check_vma=False
    )
```

profile of v0, /device:TPU:29, one launch (start us, length us, event | category | flops | bytes accessed | tf_op | source)
XLA Modules:
  0.0 813.8 jit_solution(10971161938531449910)
XLA Ops:
  6.5 0.0 copy-start.1
  6.5 0.0 all-gather.7.cloned.1.call-start
  6.5 0.7 all-gather.7.cloned.1.call-update
  7.3 0.0 all-gather.5.cloned.1.call-start
  7.3 0.2 copy-done.1
  7.5 10.8 %all-gather = bf16[1,96,4096]{2,1,0:T(8,128)(2,1)S(1)} all-gather(bf16[1,48,4096]{2,1,0:T(8,128)(2,1)S(1)} %copy-done.1), channel_id=2, replica_groups=mesh['side'=2,'group'=8,'head'=2] {'head'}, dimensions={1}, use_global_device_ids=true | all-gather | bytes 1179648 | tf_op jit(solution)/shard_map/all_gather | solution.py:19
  18.3 0.0 copy-start.2
  18.3 0.0 copy-start.3
  18.3 628.2 %all-gather.7.cloned.1.call-done = bf16[1,4096,4096]{2,1,0:T(8,128)(2,1)} async-done(((bf16[1,512,4096]{2,1,0:T(8,128)(2,1)}), bf16[1,4096,4096]{2,1,0:T(8,128)(2,1)}) %all-gather.7.cloned.1.call-update) | async-done | bytes 33554448 | tf_op jit(solution)/shard_map/all_gather | solution.py:20
  646.5 13.4 %convolution_convert_fusion = bf16[96,4096]{1,0:T(8,128)(2,1)S(1)} fusion(bf16[1,96,4096]{2,1,0:T(8,128)(2,1)S(1)} %all-gather, bf16[1,4096,4096]{2,1,0:T(8,128)(2,1)} %all-gather.7.cloned.1.call-done), kind=kOutput, calls=%fused_computation.2 | convolution fusion | flops 3221618688 | bytes 35127296 | tf_op jit(solution)/shard_map/dot_general | solution.py:26
  659.9 1.3 collective-permute-start
  661.2 2.9 collective-permute-done
  664.1 0.0 copy-start
  664.1 0.9 copy-done
  665.0 0.0 all-gather.5.cloned.1.call-update
  665.1 0.0 reduce-scatter.2.cloned.1.call-start
  665.1 0.0 copy-done.2
  665.2 0.0 copy-done.3
  665.2 0.8 fusion.41
  671.6 0.1 fusion.38
  671.8 90.0 %all-gather.5.cloned.1.call-done = bf16[768,4096]{1,0:T(8,128)(2,1)} async-done(((bf16[96,4096]{1,0:T(8,128)(2,1)}), bf16[768,4096]{1,0:T(8,128)(2,1)}) %all-gather.5.cloned.1.call-update) | async-done | bytes 6291472 | tf_op jit(solution)/shard_map/all_gather | solution.py:46
  761.8 3.4 fusion.52
  765.2 1.2 fusion.8
  766.4 0.8 fusion.9
  767.2 1.1 fusion.30
  768.3 9.9 %fusion = f32[96,4096]{1,0:T(8,128)} fusion(bf16[96,2048]{1,0:T(8,128)(2,1)S(1)} %bitcast.91, bf16[4096,4096]{1,0:T(8,128)(2,1)} %bitcast.87), kind=kOutput, calls=%fused_computation | convolution fusion | flops 1610612736 | bytes 18743296 | tf_op jit(solution)/shard_map/dot_general | solution.py:68
  778.2 0.0 reduce-scatter.2.cloned.1.call-update
  778.3 27.1 %reduce-scatter.2.cloned.1.call-done = f32[96,2048]{1,0:T(8,128)} async-done(((f32[96,4096]{1,0:T(8,128)}), f32[96,2048]{1,0:T(8,128)}) %reduce-scatter.2.cloned.1.call-update) | async-done | bytes 786448 | tf_op jit(solution)/shard_map/reduce_scatter | solution.py:71
  805.3 1.9 select_bitcast_fusion
  (6 shorter events, 0.1 us)
Async XLA Ops:
  6.5 1.0 copy-start.1
  6.5 640.0 %all-gather.7.cloned.1.call-start = ((), (), s32[]{:S(2)}) async-start(), calls=%async_computation.3 | async-start | bytes 37748736 | tf_op jit(solution)/shard_map/all_gather | solution.py:20
  7.3 754.5 %all-gather.5.cloned.1.call-start = ((), (), s32[]{:S(2)}) async-start(), calls=%async_computation.1 | async-start | bytes 7077888 | tf_op jit(solution)/shard_map/all_gather | solution.py:46
  18.3 646.8 %copy-start.2 = (s32[8,3]{0,1:T(4,128)S(1)}, s32[8,3]{0,1:T(4,128)}, u32[]{:S(2)}) copy-start(s32[8,3]{0,1:T(4,128)} %param.6) | copy-start | bytes 292
  18.3 646.9 %copy-start.3 = (s32[8,3]{0,1:T(4,128)S(1)}, s32[8,3]{0,1:T(4,128)}, u32[]{:S(2)}) copy-start(s32[8,3]{0,1:T(4,128)} %param.7) | copy-start | bytes 292
  659.9 4.2 collective-permute-start
  664.1 0.9 copy-start
  665.1 140.3 %reduce-scatter.2.cloned.1.call-start = ((), (), s32[]{:S(2)}) async-start(), calls=%async_computation.2 | async-start | bytes 2359296 | tf_op jit(solution)/shard_map/reduce_scatter | solution.py:71
Sparse Core Ops, SparseCore 0:
  8.9 637.5 all-gather.6
  665.2 96.5 all-gather.4
  778.4 26.9 reduce-scatter.1
where the time goes:
time: 816 us; the launch traced here: 814 us
  waiting for transfers between devices  749 us (92%)
  matrix products  25.6 us (3%)
  between operations  18.8 us (2%)
  blocking collectives  10.8 us (1%)
    all_gather x1, waiting for transfers between devices, on_device(): weight = lax.all_gather(pool_weight[0], 'group', axis=0, tiled=True)  628 us
    all_gather x1, waiting for transfers between devices, on_device(): piece = lax.all_gather(moved, 'group', axis=0, tiled=True)  90 us
    reduce_scatter x1, waiting for transfers between devices, on_device(): lax.psum_scatter(partial_out, 'head', scatter_dimension=1, tiled=True)  27.1 us
  transfers between devices with their start and end apart: 4, of which 4 were waited for; matrix products, arithmetic and copies ran while one was open for 0% of the time, Pallas kernels for 0%

commit v1 on v0

v1 whole, which is shorter than its diff:
```python
import functools

import jax
import jax.numpy as jnp
from jax import lax
from jax.experimental import pallas as pl
from jax.experimental.pallas import tpu as pltpu
from jax.sharding import PartitionSpec as P

HEAD_DIM = 256
LAG = 2
LANES = 128
BF = jnp.bfloat16
F32 = jnp.float32


def low_digit(groups):
    low = 1
    while low * low * 4 <= groups:
        low *= 2
    return low


def aligned(index, size):
    return pl.ds(pl.multiple_of(index * size, size), size)


def kernel(dims, pick_ref, mask_ref, x_ref, w_hbm, out_ref, w, xg, xp, part, ysend, yrecv, zown, zsend, zrecv,
           proj, kv, attg, pout, osend, orecv, wsem, lsem, xss, xrs, fss, frs, yss, yrs, zss, zrs, kss, krs,
           ass, ars, bss, brs, oss, ors):
    ng, nh, nl, nz, rows, mem, kc, wide, ch, req = dims
    nc = wide // ch
    q_req = mem // req
    side = lax.axis_index("side")
    g = lax.axis_index("group")
    h = lax.axis_index("head")
    z = g // nl
    y = g % nl
    scale = 1.0 / HEAD_DIM**0.5

    def remote(src, dst, ssem, rsem, to):
        return pltpu.make_async_remote_copy(
            src_ref=src, dst_ref=dst, send_sem=ssem, recv_sem=rsem, device_id=to,
            device_id_type=pl.DeviceIdType.MESH)

    load_w = pltpu.make_async_copy(w_hbm.at[0], w, wsem)
    load_w.start()

    barrier = pltpu.get_barrier_semaphore()
    others = ng * nh - 1
    me = g * nh + h

    def greet(k, carry):
        to = (me + 1 + k) % (ng * nh)
        pl.semaphore_signal(barrier, inc=1, device_id=(side, to // nh, to % nh), device_id_type=pl.DeviceIdType.MESH)
        return carry

    lax.fori_loop(0, others, greet, 0)
    pl.semaphore_signal(barrier, inc=1, device_id=(1 - side, g, h), device_id_type=pl.DeviceIdType.MESH)
    pl.semaphore_wait(barrier, others + 1)

    def row_slot(gg, hh):
        return aligned(gg * nh + hh, rows)

    own_cols = x_ref.at[:, aligned(g, kc)]
    place = pltpu.make_async_copy(own_cols, xg.at[row_slot(g, h)], lsem)
    place.start()

    def x_send(k):
        to = (g + k) % ng
        return remote(x_ref.at[:, aligned(to, kc)], xg.at[row_slot(g, h)], xss.at[k], xrs.at[k], (side, to, h))

    def x_forward(k, j):
        source = (g - k + ng) % ng
        src = own_cols if k == 0 else xg.at[row_slot(source, h)]
        return remote(src, xg.at[row_slot(source, h)], fss.at[k, j], frs.at[k, j], (side, g, (h + j) % nh))

    for k in range(1, ng):
        x_send(k).start()
    for j in range(1, nh):
        x_forward(0, j).start()
    for k in range(1, ng):
        x_send(k).wait_recv()
        for j in range(1, nh):
            x_forward(k, j).start()
    place.wait()
    for k in range(ng):
        for j in range(1, nh):
            x_forward(k, j).wait_recv()

    def chosen(source_ref, group, slot):
        total = None
        for source in range(ng):
            keep = jnp.broadcast_to(pick_ref[group * req + slot, source:source + 1, :], (q_req, LANES)).astype(BF)
            keep = jnp.concatenate([keep] * (kc // LANES), axis=1)
            term = source_ref[aligned(source * req + slot, q_req), :].astype(BF) * keep
            total = term if total is None else total + term
        return total

    def order(block, carry):
        at, slot = block // req, block % req
        group = (at % nz) * nl + at // nz

        @pl.when(side == 1)
        def _():
            xp[aligned(block, q_req), :] = chosen(xg, group, slot)

        @pl.when(side == 0)
        def _():
            xp[aligned(block, q_req), :] = xg[aligned(group * req + slot, q_req), :]

        return carry

    lax.fori_loop(0, ng * req, order, 0)
    load_w.wait()

    half = nz * mem

    def y_copy(c, k):
        to = z * nl + (y + k) % nl
        return remote(ysend.at[c, k - 1], yrecv.at[c, k - 1], yss.at[c, k - 1], yrs.at[c, k - 1], (side, to, h))

    def z_copy(c, k):
        to = ((z + k) % nz) * nl + y
        return remote(zsend.at[c, k - 1], zrecv.at[c, k - 1], zss.at[c, k - 1], zrs.at[c, k - 1], (side, to, h))

    def kv_copy(c):
        return remote(proj.at[c], kv.at[c], kss.at[c], krs.at[c], (1 - side, g, h))

    chunks = jnp.where(side == 0, 2 * nc, nc)

    def product(c, carry):
        col = jnp.where(side == 0, (c % 2) * nc + c // 2, c)
        block = w[:, aligned(col, ch)]
        for k in range(1, nl):
            got = jnp.dot(xp[aligned((y + k) % nl, half), :], block, preferred_element_type=F32)
            ysend[c, k - 1] = got.astype(BF)
            y_copy(c, k).start()
        part[c] = jnp.dot(xp[aligned(y, half), :], block, preferred_element_type=F32)
        return carry

    lax.fori_loop(0, chunks, product, 0)

    def reduce_y(c):
        for k in range(1, nl):
            y_copy(c, k).wait_recv()
        for k in list(range(1, nz)) + [0]:
            sel = aligned((z + k) % nz, mem)
            total = part[c, sel, :]
            for kk in range(1, nl):
                total = total + yrecv[c, kk - 1, sel, :].astype(F32)
            if k:
                zsend[c, k - 1] = total.astype(BF)
                z_copy(c, k).start()
            else:
                zown[c] = total

    def reduce_z(c):
        total = zown[c]
        for k in range(1, nz):
            z_copy(c, k).wait_recv()
            total = total + zrecv[c, k - 1].astype(F32)
        proj[c] = total.astype(BF)

        @pl.when(side == 0)
        def _():
            kv_copy(c).start()

            @pl.when(c % 2 == 0)
            def _():
                out_ref[:, aligned(c // 2, ch)] = proj[c]

    def reduce(i, carry):
        @pl.when(i < chunks)
        def _():
            reduce_y(i)

        @pl.when(i >= LAG)
        def _():
            reduce_z(i - LAG)

        return carry

    lax.fori_loop(0, chunks + LAG, reduce, 0)

    def az_copy(c, k):
        to = ((z + k) % nz) * nl + y
        here = attg.at[c, aligned(g, mem)]
        return remote(here, here, ass.at[c, k], ars.at[c, k], (side, to, h))

    def ay_copy(c, k, j):
        source = ((z - k + nz) % nz) * nl + y
        here = attg.at[c, aligned(source, mem)]
        return remote(here, here, bss.at[c, k, j], brs.at[c, k, j], (side, z * nl + (y + j) % nl, h))

    def attend(c):
        for b in range(2):
            remote(proj.at[2 * c + b], kv.at[2 * c + b], kss.at[2 * c + b], krs.at[2 * c + b],
                   (1 - side, g, h)).wait_recv()
        allowed = mask_ref[...] == 1
        for e in range(ch // HEAD_DIM):
            cols = slice(e * HEAD_DIM, (e + 1) * HEAD_DIM)
            scores = lax.dot_general(proj[c, :, cols], kv[2 * c, :, cols], (((1,), (1,)), ((), ())),
                                     preferred_element_type=F32) * scale
            scores = jnp.where(allowed, scores, -1e30)
            peak = jnp.max(scores, axis=-1, keepdims=True)
            expo = jnp.where(allowed, jnp.exp(scores - peak), 0.0)
            total = jnp.sum(expo, axis=-1, keepdims=True)
            mixed = jnp.dot(expo.astype(BF), kv[2 * c + 1, :, cols], preferred_element_type=F32) / total
            attg[c, aligned(g, mem), cols] = mixed.astype(BF)
        for k in range(1, nz):
            az_copy(c, k).start()
        for j in range(1, nl):
            ay_copy(c, 0, j).start()

    def forward(c):
        for k in range(1, nz):
            az_copy(c, k).wait_recv()
            for j in range(1, nl):
                ay_copy(c, k, j).start()

    def out_product(c):
        for k in range(nz):
            for j in range(1, nl):
                ay_copy(c, k, j).wait_recv()
        block = w[:, aligned(nc + c, ch)]

        def rows_part(i, carry):
            sel = aligned(i, half)
            got = lax.dot_general(attg[c, sel, :], block, (((1,), (1,)), ((), ())), preferred_element_type=F32)
            pout[sel, :] = jnp.where(c == 0, got, pout[sel, :] + got)
            return carry

        lax.fori_loop(0, nl, rows_part, 0)

    per_head = ng // nh
    home = g // per_head
    slot_here = (g % per_head) * nh + h

    def o_copy(k):
        to = (g + k) % ng
        return remote(osend.at[k], orecv.at[slot_here], oss.at[k], ors.at[slot_here], (side, to, home))

    own_out = pltpu.make_async_copy(osend.at[0], orecv.at[slot_here], ors.at[slot_here])

    @pl.when(side == 1)
    def _():
        pout[...] = jnp.zeros_like(pout)

        def step(i, carry):
            @pl.when(i < nc)
            def _():
                attend(i)

            @pl.when((i >= 1) & (i <= nc))
            def _():
                forward(i - 1)

            @pl.when(i >= 2)
            def _():
                out_product(i - 2)

            return carry

        lax.fori_loop(0, nc + 2, step, 0)

        for k in list(range(1, ng)) + [0]:
            to = (g + k) % ng
            for slot in range(req):
                osend[k, slot * q_req:(slot + 1) * q_req, :] = chosen(pout, to, slot)
            if k:
                o_copy(k).start()
            else:
                @pl.when(h == home)
                def _():
                    own_out.start()

                @pl.when(h != home)
                def _():
                    o_copy(0).start()
        for f in range(per_head):
            total = None
            for hh in range(nh):
                at = f * nh + hh
                pltpu.make_async_copy(osend.at[0], orecv.at[at], ors.at[at]).wait()
                term = orecv[at].astype(F32)
                total = term if total is None else total + term
            out_ref[:, f * kc:(f + 1) * kc] = total.astype(BF)

    for k in range(1, ng):
        x_send(k).wait_send()
    for k in range(ng):
        for j in range(1, nh):
            x_forward(k, j).wait_send()

    def drain(c, carry):
        for k in range(1, nl):
            y_copy(c, k).wait_send()
        for k in range(1, nz):
            z_copy(c, k).wait_send()

        @pl.when(side == 0)
        def _():
            kv_copy(c).wait_send()

        return carry

    lax.fori_loop(0, chunks, drain, 0)

    @pl.when(side == 1)
    def _():
        def drain_out(c, carry):
            for k in range(1, nz):
                az_copy(c, k).wait_send()
            for k in range(nz):
                for j in range(1, nl):
                    ay_copy(c, k, j).wait_send()
            return carry

        lax.fori_loop(0, nc, drain_out, 0)
        for k in range(1, ng):
            o_copy(k).wait_send()

        @pl.when(h != home)
        def _():
            o_copy(0).wait_send()


def on_device(pool_rows, pool_weight, lengths, owner):
    ng, nh = lax.axis_size("group"), lax.axis_size("head")
    nl = low_digit(ng)
    nz = ng // nl
    rows, depth = pool_rows.shape[1:]
    mem = rows * nh
    kc = pool_weight.shape[1]
    wide = pool_weight.shape[2] // 2
    ch = 2 * HEAD_DIM if wide % (2 * HEAD_DIM) == 0 else HEAD_DIM
    nc = wide // ch
    req = lengths.shape[1]
    total = mem * ng
    dims = (ng, nh, nl, nz, rows, mem, kc, wide, ch, req)
    pick = owner.reshape(ng * req, 1) == jnp.arange(ng, dtype=jnp.int32)[None, :]
    pick = jnp.broadcast_to(pick[:, :, None], (ng * req, ng, LANES)).astype(F32)
    count = lax.dynamic_index_in_dim(lengths, lax.axis_index("group"), 0, keepdims=False)
    row_slot = jnp.arange(mem, dtype=jnp.int32)[:, None] // (mem // req)
    key = jnp.arange(mem, dtype=jnp.int32)[None, :]
    mask = jnp.zeros((mem, mem), jnp.int32)
    first = jnp.int32(0)
    for slot in range(req):
        mask = jnp.where((row_slot == slot) & (key >= first) & (key < first + count[slot]), 1, mask)
        first = first + count[slot]
    dma = pltpu.SemaphoreType.DMA
    ly, lz = max(nl - 1, 1), max(nz - 1, 1)
    out = pl.pallas_call(
        functools.partial(kernel, dims),
        out_shape=jax.ShapeDtypeStruct((mem, wide), BF),
        in_specs=[
            pl.BlockSpec(memory_space=pltpu.VMEM),
            pl.BlockSpec(memory_space=pltpu.VMEM),
            pl.BlockSpec(memory_space=pltpu.VMEM),
            pl.BlockSpec(memory_space=pl.ANY),
        ],
        out_specs=pl.BlockSpec(memory_space=pltpu.VMEM),
        scratch_shapes=[
            pltpu.VMEM((kc, 2 * wide), BF),
            pltpu.VMEM((total, kc), BF),
            pltpu.VMEM((total, kc), BF),
            pltpu.VMEM((2 * nc, nz * mem, ch), F32),
            pltpu.VMEM((2 * nc, ly, nz * mem, ch), BF),
            pltpu.VMEM((2 * nc, ly, nz * mem, ch), BF),
            pltpu.VMEM((2 * nc, mem, ch), F32),
            pltpu.VMEM((2 * nc, lz, mem, ch), BF),
            pltpu.VMEM((2 * nc, lz, mem, ch), BF),
            pltpu.VMEM((2 * nc, mem, ch), BF),
            pltpu.VMEM((2 * nc, mem, ch), BF),
            pltpu.VMEM((nc, total, ch), BF),
            pltpu.VMEM((total, kc), F32),
            pltpu.VMEM((ng, mem, kc), BF),
            pltpu.VMEM((ng, mem, kc), BF),
            dma, dma, dma((ng,)), dma((ng,)), dma((ng, nh)), dma((ng, nh)),
            dma((2 * nc, ly)), dma((2 * nc, ly)), dma((2 * nc, lz)), dma((2 * nc, lz)),
            dma((2 * nc,)), dma((2 * nc,)),
            dma((nc, nz)), dma((nc, nz)), dma((nc, nz, nl)), dma((nc, nz, nl)),
            dma((ng,)), dma((ng,)),
        ],
        compiler_params=pltpu.CompilerParams(
            collective_id=0, has_side_effects=True, vmem_limit_bytes=67043328),
    )(pick, mask, pool_rows[0], pool_weight)
    return out[None]


def solution(mesh):
    placed = (P("side", ("group", "head"), None), P("side", "group", "head"), P(), P())
    return jax.shard_map(
        on_device, mesh=mesh, in_specs=placed, out_specs=P("side", "group", "head"), check_vma=False
    )
```

time: 816 us -> 132 us (0.16)
  waiting for transfers between devices: 749 us -> 0 us
  Pallas kernels: 0 us -> 123 us
  matrix products: 25.6 us -> 0 us
  between operations: 18.8 us -> 1.86 us
  blocking collectives: 10.8 us -> 0 us
    all_gather x2 -> x0, waiting for transfers between devices: 718 us -> none  [the longest x1 628 us: on_device(): weight = lax.all_gather(pool_weight[0], 'group', axis=0, tiled=True)]
    pallas_call x0 -> x1, Pallas kernels: none -> 123 us  [on_device(): pl.pallas_call(functools.partial(kernel, dims), out_shape=jax.ShapeDtypeS...]
    reduce_scatter x1 -> x0, waiting for transfers between devices: 27.1 us -> none  [on_device(): lax.psum_scatter(partial_out, 'head', scatter_dimension=1, tiled=True)]
    dot_general x4 -> x0, matrix products: 25.6 us -> none  [the longest x1 13.4 us: on_device(): jnp.dot(gathered, weight, preferred_element_type=jnp.float32)]
    all_gather x1 -> x0, blocking collectives: 10.8 us -> none  [on_device(): gathered = lax.all_gather(pool_rows[0], 'head', axis=0, tiled=True)]
  transfers between devices with their start and end apart: 4 -> 0, of which waited for: 4 -> 0; matrix products, arithmetic and copies ran while one was open for 0% -> 0% of each run, Pallas kernels for 0% -> 0%
where the time goes in v1:
time: 132 us; the launch traced here: 131 us
  Pallas kernels  123 us (93%)
  local copies, waits for them, and re-layouts  4.61 us (3%)
  between operations  1.86 us (1%)
  other arithmetic  1.38 us (1%)
    pallas_call x1, Pallas kernels, on_device(): pl.pallas_call(functools.partial(kernel, dims), out_shape=jax.ShapeDtypeS...  123 us

profile of v1, /device:TPU:29, one launch (start us, length us, event | category | flops | bytes accessed | tf_op | source)
XLA Modules:
  0.0 131.2 jit_solution(6413973279939023962)
XLA Ops:
  0.0 0.8 constant_dynamic-slice_fusion
  0.8 0.5 fusion.1
  3.1 0.6 iota_compare_fusion.1
  3.7 0.8 copy.6
  4.5 0.1 eq.48
  4.6 0.1 fusion
  4.6 0.7 select_select_fusion.mask_ref
  5.4 0.7 broadcast_in_dim.21.pick_ref
  6.1 123.4 %shard_map.46 = bf16[96,2048]{1,0:T(8,128)(2,1)} custom-call(f32[24,8,128]{2,1,0:T(8,128)} %broadcast_in_dim.21.pick_ref, s32[96,96]{1,0:T(8,128)} %select_select_fusion.mask_ref, bf16[48,4096]{1,0:T(8,128)(2,1)} %bitcast.6, bf16[1,512,4096]{2,1,0:T(8,128)(2,1)} %w_hbm.1), custom_call_target="tpu_custom_call" | custom-call | tf_op jit(solution)/shard_map/pallas_call | solution.py:354
  129.5 1.8 %copy.8 = bf16[1,96,2048]{2,1,0:T(8,128)(2,1)} copy(bf16[1,96,2048]{2,1,0:T(8,128)(2,1)} %bitcast.5) | data formatting | bytes 786432
  (3 shorter events, 0.0 us)

commit v2 on v1

v2 whole, which is shorter than its diff:
```python
import functools

import jax
import jax.numpy as jnp
from jax import lax
from jax.experimental import pallas as pl
from jax.experimental.pallas import tpu as pltpu
from jax.sharding import PartitionSpec as P

HEAD_DIM = 256
LAG = 1
EARLY = 2
CELL = 4
LANES = 128
BF = jnp.bfloat16
F32 = jnp.float32
MESH = pl.DeviceIdType.MESH


def aligned(index, size):
    return pl.ds(pl.multiple_of(index * size, size), size)


def kernel(dims, owner_ref, lengths_ref, x_ref, w_hbm, out_ref, ow, wv, xg, prod, zown, zsend, zrecv, proj, kv, kx,
           attg, pout, osend, omid, orecv, osem, wss, wrs, xss, xrs, lss, lrs, hss, hrs, zss, zrs, kss, krs,
           yss, yrs, ass, ars, bss, brs, oss, ors, pss, prs):
    ng, nh, nl, nz, rows, mem, kc, wide, ch, req = dims
    part = wide // nl
    nc = part // ch
    q_req = mem // req
    cell = nl * mem
    depth = nl * kc
    side = lax.axis_index("side")
    g = lax.axis_index("group")
    h = lax.axis_index("head")
    z = g // nl
    lo = g % nl
    scale = 1.0 / HEAD_DIM**0.5
    chunks = jnp.where(side == 0, 2 * nc, nc)

    def remote(src, dst, ssem, rsem, to):
        return pltpu.make_async_remote_copy(
            src_ref=src, dst_ref=dst, send_sem=ssem, recv_sem=rsem, device_id=to, device_id_type=MESH)

    def at(zz, ll):
        return (side, ((zz + nz) % nz) * nl + (ll + nl) % nl, h)

    def w_cols(i, ll):
        second = jnp.where(side == 0, i % 2, 0)
        step = jnp.where(side == 0, i // 2, i)
        return aligned(second * (wide // ch) + ll * nc + step, ch)

    def w_copy(i, k):
        to = (lo + k) % nl
        return remote(w_hbm.at[0, :, w_cols(i, to)], wv.at[i, aligned(lo, kc)], wss.at[i, k], wrs.at[i, k], at(z, to))

    def w_own(i):
        return pltpu.make_async_copy(w_hbm.at[0, :, w_cols(i, lo)], wv.at[i, aligned(lo, kc)], wrs.at[i, 0])

    load_out = pltpu.make_async_copy(w_hbm.at[0, :, pl.ds(wide, wide)], ow, osem)

    def load_own(i, carry):
        w_own(i).start()
        return carry

    lax.fori_loop(0, chunks, load_own, 0)

    @pl.when(side == 1)
    def _():
        load_out.start()

    barrier = pltpu.get_barrier_semaphore()
    others = ng * nh - 1
    me = g * nh + h

    def greet(k, carry):
        to = (me + 1 + k) % (ng * nh)
        pl.semaphore_signal(barrier, inc=1, device_id=(side, to // nh, to % nh), device_id_type=MESH)
        return carry

    lax.fori_loop(0, others, greet, 0)
    pl.semaphore_signal(barrier, inc=1, device_id=(1 - side, g, h), device_id_type=MESH)
    pl.semaphore_wait(barrier, others + 1)

    def start_w(i, carry):
        for k in range(1, nl):
            w_copy(i, k).start()
        return carry

    def row_slot(gg, hh):
        return aligned(gg * nh + hh, rows)

    own_cols = x_ref.at[0, :, aligned(z, depth)]
    place = pltpu.make_async_copy(own_cols, xg.at[row_slot(g, h)], xrs.at[0])
    place.start()

    def x_high(k):
        to = (z + k) % nz
        return remote(x_ref.at[0, :, aligned(to, depth)], xg.at[row_slot(g, h)], xss.at[k], xrs.at[k], at(to, lo))

    def block_of(k, j):
        source = ((z - k + nz) % nz) * nl + (lo - j + nl) % nl
        dst = xg.at[row_slot(source, h)]
        return (own_cols if k == 0 and j == 0 else dst), dst

    def x_low(k, j):
        src, dst = block_of(k, 0)
        return remote(src, dst, lss.at[k, j], lrs.at[k, j], at(z, lo + j))

    def x_head(k, j, m):
        src, dst = block_of(k, j)
        return remote(src, dst, hss.at[k, j, m], hrs.at[k, j, m], (side, g, (h + m) % nh))

    for k in range(1, nz):
        x_high(k).start()
    for k in range(nz):
        if k:
            x_high(k).wait_recv()
        for j in range(1, nl):
            x_low(k, j).start()
        for m in range(1, nh):
            x_head(k, 0, m).start()
    lax.fori_loop(0, jnp.minimum(EARLY, chunks), start_w, 0)
    for k in range(nz):
        for j in range(1, nl):
            x_low(k, j).wait_recv()
            for m in range(1, nh):
                x_head(k, j, m).start()
    lax.fori_loop(jnp.minimum(EARLY, chunks), chunks, start_w, 0)
    place.wait()
    for k in range(nz):
        for j in range(nl):
            for m in range(1, nh):
                x_head(k, j, m).wait_recv()

    def chosen(source_ref, group, slot, lanes):
        which = jnp.broadcast_to(owner_ref[pl.ds(group, 1), slot:slot + 1], (q_req, LANES))
        total = jnp.zeros((q_req, LANES), F32)
        for source in range(ng):
            start = (source * req + slot) * q_req
            total = jnp.where(which == source, source_ref[start:start + q_req, lanes], total)
        return total

    def z_copy(c, k):
        return remote(zsend.at[c, k - 1], zrecv.at[c, k - 1], zss.at[c, k - 1], zrs.at[c, k - 1], at(z + k, lo))

    def kv_copy(c):
        return remote(proj.at[c], kv.at[c], kss.at[c], krs.at[c], (1 - side, g, h))

    def key_copy(c, k):
        to = (lo + k) % nl
        return remote(proj.at[2 * c, aligned(to, mem)], kx.at[c, lo], yss.at[c, k], yrs.at[c, k], at(z, to))

    def product(c):
        w_own(c).wait()
        for k in range(1, nl):
            w_copy(c, k).wait_recv()

        def rows_part(i, carry):
            sel = aligned(i, cell)
            prod[sel, :] = jnp.dot(xg[sel, :], wv[c], preferred_element_type=F32)
            return carry

        lax.fori_loop(0, nz, rows_part, 0)
        for k in list(range(1, nz)) + [0]:
            to = (z + k) % nz

            @pl.when(side == 0)
            def _():
                if k:
                    zsend[c, k - 1] = prod[aligned(to, cell), :].astype(BF)
                else:
                    zown[c] = prod[aligned(to, cell), :]

            @pl.when(side == 1)
            def _():
                def member(ll, carry):
                    for slot in range(req):
                        put = aligned(ll * req + slot, q_req)
                        for lane in range(ch // LANES):
                            lanes = slice(lane * LANES, (lane + 1) * LANES)
                            got = chosen(prod, to * nl + ll, slot, lanes)
                            if k:
                                zsend[c, k - 1, put, lanes] = got.astype(BF)
                            else:
                                zown[c, put, lanes] = got
                    return carry

                lax.fori_loop(0, nl, member, 0)

            if k:
                z_copy(c, k).start()

    def reduce_z(c):
        total = zown[c]
        for k in range(1, nz):
            z_copy(c, k).wait_recv()
            total = total + zrecv[c, k - 1].astype(F32)
        proj[c] = total.astype(BF)

        @pl.when(side == 0)
        def _():
            kv_copy(c).start()

            @pl.when(c % 2 == 0)
            def _():
                for k in range(1, nl):
                    key_copy(c // 2, k).start()
                out_ref[:, aligned(lo * nc + c // 2, ch)] = proj[c, aligned(lo, mem), :]

    def reduce(i, carry):
        @pl.when(i < chunks)
        def _():
            product(i)

        @pl.when(i >= LAG)
        def _():
            reduce_z(i - LAG)

        return carry

    lax.fori_loop(0, chunks + LAG, reduce, 0)

    def az_copy(c, k):
        here = attg.at[lo * nc + c, aligned(z, cell)]
        return remote(here, here, ass.at[c, k], ars.at[c, k], at(z + k, lo))

    def ay_copy(c, k, j):
        here = attg.at[lo * nc + c, aligned((z - k + nz) % nz, cell)]
        return remote(here, here, bss.at[c, k, j], brs.at[c, k, j], at(z, lo + j))

    def allowed_keys():
        row = lax.broadcasted_iota(jnp.int32, (cell, cell), 0)
        key = lax.broadcasted_iota(jnp.int32, (cell, cell), 1)
        slots = row // q_req
        lower = jnp.zeros((cell, cell), jnp.int32)
        upper = jnp.zeros((cell, cell), jnp.int32)
        for ll in range(nl):
            first = jnp.full((1, 1), ll * mem, jnp.int32)
            for slot in range(req):
                here = slots == ll * req + slot
                last = first + lengths_ref[pl.ds(z * nl + ll, 1), slot:slot + 1]
                lower = jnp.where(here, jnp.broadcast_to(first, (cell, cell)), lower)
                upper = jnp.where(here, jnp.broadcast_to(last, (cell, cell)), upper)
                first = last
        return (key >= lower) & (key < upper)

    def attend(c):
        for b in range(2):
            kv_copy(2 * c + b).wait_recv()
        allowed = allowed_keys()
        for e in range(ch // HEAD_DIM):
            cols = slice(e * HEAD_DIM, (e + 1) * HEAD_DIM)
            scores = lax.dot_general(proj[c, :, cols], kv[2 * c, :, cols], (((1,), (1,)), ((), ())),
                                     preferred_element_type=F32) * scale
            scores = jnp.where(allowed, scores, -1e30)
            peak = jnp.max(scores, axis=-1, keepdims=True)
            expo = jnp.where(allowed, jnp.exp(scores - peak), 0.0)
            total = jnp.sum(expo, axis=-1, keepdims=True)
            mixed = jnp.dot(expo.astype(BF), kv[2 * c + 1, :, cols], preferred_element_type=F32) / total
            attg[lo * nc + c, aligned(z, cell), cols] = mixed.astype(BF)
        for k in range(1, nz):
            az_copy(c, k).start()
        for j in range(1, nl):
            ay_copy(c, 0, j).start()

    def forward(c):
        for k in range(1, nz):
            az_copy(c, k).wait_recv()
            for j in range(1, nl):
                ay_copy(c, k, j).start()

    def out_product(c):
        for j in range(nl):
            if j:
                for k in range(nz):
                    ay_copy(c, k, j).wait_recv()
            index = ((lo - j + nl) % nl) * nc + c
            block = ow[:, aligned(index, ch)]

            def rows_part(i, carry):
                sel = aligned(i, cell)
                got = lax.dot_general(attg[index, sel, :], block, (((1,), (1,)), ((), ())),
                                      preferred_element_type=F32)
                pout[sel, :] = pout[sel, :] + got
                return carry

            lax.fori_loop(0, nz, rows_part, 0)

    per_head = ng // nh

    def o_copy(k):
        to = (g + k) % ng
        return remote(osend.at[k], omid.at[g], oss.at[k], ors.at[k], (side, to, h))

    def o_head(gg):
        slot = (gg % per_head) * nh + h
        return remote(omid.at[gg], orecv.at[slot], pss.at[gg], prs.at[slot], (side, g, gg // per_head))

    @pl.when(side == 1)
    def _():
        pout[...] = jnp.zeros_like(pout)
        load_out.wait()

        def step(i, carry):
            @pl.when(i < nc)
            def _():
                attend(i)

            @pl.when((i >= 1) & (i <= nc))
            def _():
                forward(i - 1)

            @pl.when(i >= 2)
            def _():
                out_product(i - 2)

            return carry

        lax.fori_loop(0, nc + 2, step, 0)

        def spread(i, carry):
            k = (i + 1) % ng
            to = (g + k) % ng
            for slot in range(req):
                for lane in range(kc // LANES):
                    lanes = slice(lane * LANES, (lane + 1) * LANES)
                    osend[k, slot * q_req:(slot + 1) * q_req, lanes] = chosen(pout, to, slot, lanes).astype(BF)

            @pl.when(k > 0)
            def _():
                o_copy(k).start()

            return carry

        lax.fori_loop(0, ng, spread, 0)
        omid[g] = osend[0]

        def pass_on(k, carry):
            gg = (g - k + ng) % ng

            @pl.when(k > 0)
            def _():
                o_copy(k).wait_recv()

            @pl.when(gg // per_head != h)
            def _():
                o_head(gg).start()

            return carry

        lax.fori_loop(0, ng, pass_on, 0)
        for f in range(per_head):
            total = omid[h * per_head + f].astype(F32)
            for m in range(1, nh):
                slot = f * nh + (h + m) % nh
                remote(omid.at[0], orecv.at[slot], pss.at[0], prs.at[slot], (side, g, (h + m) % nh)).wait_recv()
                total = total + orecv[slot].astype(F32)
            out_ref[:, f * kc:(f + 1) * kc] = total.astype(BF)

    @pl.when(side == 0)
    def _():
        for c in range(nc):
            for k in range(1, nl):
                key_copy(c, k).wait_recv()
                source = (lo - k + nl) % nl
                out_ref[:, aligned(source * nc + c, ch)] = kx[c, source]

    for k in range(nz):
        if k:
            x_high(k).wait_send()
        for j in range(nl):
            if j:
                x_low(k, j).wait_send()
            for m in range(1, nh):
                x_head(k, j, m).wait_send()

    def drain(c, carry):
        for k in range(1, nl):
            w_copy(c, k).wait_send()
        for k in range(1, nz):
            z_copy(c, k).wait_send()

        @pl.when(side == 0)
        def _():
            kv_copy(c).wait_send()

        return carry

    lax.fori_loop(0, chunks, drain, 0)

    @pl.when(side == 0)
    def _():
        for c in range(nc):
            for k in range(1, nl):
                key_copy(c, k).wait_send()

    @pl.when(side == 1)
    def _():
        def drain_out(c, carry):
            for k in range(1, nz):
                az_copy(c, k).wait_send()
            for k in range(nz):
                for j in range(1, nl):
                    ay_copy(c, k, j).wait_send()
            return carry

        lax.fori_loop(0, nc, drain_out, 0)

        def drain_last(k, carry):
            gg = (g - k + ng) % ng

            @pl.when(k > 0)
            def _():
                o_copy(k).wait_send()

            @pl.when(gg // per_head != h)
            def _():
                o_head(gg).wait_send()

            return carry

        lax.fori_loop(0, ng, drain_last, 0)


def on_device(pool_rows, pool_weight, lengths, owner):
    ng, nh = lax.axis_size("group"), lax.axis_size("head")
    rows = pool_rows.shape[1]
    mem = rows * nh
    kc = pool_weight.shape[1]
    wide = pool_weight.shape[2] // 2
    nl = min(CELL, wide // HEAD_DIM)
    nz = ng // nl
    ch = HEAD_DIM
    nc = wide // nl // ch
    req = lengths.shape[1]
    total = mem * ng
    cell = nl * mem
    dims = (ng, nh, nl, nz, rows, mem, kc, wide, ch, req)
    dma = pltpu.SemaphoreType.DMA
    lz = max(nz - 1, 1)
    out = pl.pallas_call(
        functools.partial(kernel, dims),
        out_shape=jax.ShapeDtypeStruct((mem, wide), BF),
        in_specs=[
            pl.BlockSpec(memory_space=pltpu.VMEM),
            pl.BlockSpec(memory_space=pltpu.VMEM),
            pl.BlockSpec(memory_space=pltpu.VMEM),
            pl.BlockSpec(memory_space=pl.ANY),
        ],
        out_specs=pl.BlockSpec(memory_space=pltpu.VMEM),
        scratch_shapes=[
            pltpu.VMEM((kc, wide), BF),
            pltpu.VMEM((2 * nc, nl * kc, ch), BF),
            pltpu.VMEM((total, nl * kc), BF),
            pltpu.VMEM((total, ch), F32),
            pltpu.VMEM((2 * nc, cell, ch), F32),
            pltpu.VMEM((2 * nc, lz, cell, ch), BF),
            pltpu.VMEM((2 * nc, lz, cell, ch), BF),
            pltpu.VMEM((2 * nc, cell, ch), BF),
            pltpu.VMEM((2 * nc, cell, ch), BF),
            pltpu.VMEM((nc, nl, mem, ch), BF),
            pltpu.VMEM((nl * nc, total, ch), BF),
            pltpu.VMEM((total, kc), F32),
            pltpu.VMEM((ng, mem, kc), BF),
            pltpu.VMEM((ng, mem, kc), BF),
            pltpu.VMEM((ng, mem, kc), BF),
            dma, dma((2 * nc, nl)), dma((2 * nc, nl)), dma((nz,)), dma((nz,)), dma((nz, nl)), dma((nz, nl)),
            dma((nz, nl, nh)), dma((nz, nl, nh)), dma((2 * nc, lz)), dma((2 * nc, lz)),
            dma((2 * nc,)), dma((2 * nc,)), dma((nc, nl)), dma((nc, nl)),
            dma((nc, nz)), dma((nc, nz)), dma((nc, nz, nl)), dma((nc, nz, nl)),
            dma((ng,)), dma((ng,)), dma((ng,)), dma((ng,)),
        ],
        compiler_params=pltpu.CompilerParams(
            collective_id=0, has_side_effects=True, vmem_limit_bytes=67043328),
    )(owner, lengths, pool_rows, pool_weight)
    return out[None]


def solution(mesh):
    placed = (P("side", ("group", "head"), None), P("side", "group", "head"), P(), P())
    return jax.shard_map(
        on_device, mesh=mesh, in_specs=placed, out_specs=P("side", "group", "head"), check_vma=False
    )
```

time: 132 us -> 128 us (0.970)
  between operations: 1.86 us -> 0.01 us
  other arithmetic: 1.38 us -> 0 us
    unnamed x2 -> x3, local copies, waits for them, and re-layouts: 2.53 us -> 4.45 us
where the time goes in v2:
time: 128 us; the launch traced here: 127 us
  Pallas kernels  123 us (96%)
  local copies, waits for them, and re-layouts  4.45 us (3%)
    pallas_call x1, Pallas kernels, on_device(): pl.pallas_call(functools.partial(kernel, dims), out_shape=jax.ShapeDtypeS...  123 us
    unnamed x3, local copies, waits for them, and re-layouts  4.45 us

profile of v2, /device:TPU:29, one launch (start us, length us, event | category | flops | bytes accessed | tf_op | source)
XLA Modules:
  0.0 127.3 jit_solution(4510283267679998043)
XLA Ops:
  0.0 1.3 %copy.6.lengths_ref = s32[8,3]{1,0:T(8,128)} copy(s32[8,3]{0,1:T(4,128)} %param.6) | data formatting | bytes 192 | tf_op args[2]
  1.3 1.3 %copy.5.owner_ref = s32[8,3]{1,0:T(8,128)} copy(s32[8,3]{0,1:T(4,128)} %param.7) | data formatting | bytes 192 | tf_op args[3]
  2.7 122.8 %shard_map.46 = bf16[96,2048]{1,0:T(8,128)(2,1)} custom-call(s32[8,3]{1,0:T(8,128)} %copy.5.owner_ref, s32[8,3]{1,0:T(8,128)} %copy.6.lengths_ref, bf16[1,48,4096]{2,1,0:T(8,128)(2,1)} %x_ref.1, bf16[1,512,4096]{2,1,0:T(8,128)(2,1)} %w_hbm.1), custom_call_target="tpu_custom_call" | custom-call | tf_op jit(solution)/shard_map/pallas_call | solution.py:442
  125.5 1.8 %copy.8 = bf16[1,96,2048]{2,1,0:T(8,128)(2,1)} copy(bf16[1,96,2048]{2,1,0:T(8,128)(2,1)} %bitcast.1) | data formatting | bytes 786432
